TPU v7x, 32 devices: a whole 2x2x4 slice. The times are simulated.
32 devices in a mesh: row: 4 (over y, x), col: 8 (over z, core).
Axes of the slice: x: 2, y: 2, z: 4, core: 2. Of those that a mesh axis runs over, the one named last changes fastest.
Arguments:
- activations: bfloat16 [512, 16384], P('col', 'row'), may hold values from -6 to 6
- grad_output: bfloat16 [512, 16384], P('col', 'row'), may hold values from -6 to 6
- gate_pre: bfloat16 [512, 8192], P('row', 'col'), may hold values from -8 to 8
- up_pre: bfloat16 [512, 8192], P('row', 'col'), may hold values from -6 to 6
- w_gate: bfloat16 [16384, 8192], P('row', 'col'), may hold values from -0.046875 to 0.046875
- w_up: bfloat16 [16384, 8192], P('row', 'col'), may hold values from -0.046875 to 0.046875
- w_down: bfloat16 [8192, 16384], P('col', 'row'), may hold values from -0.0625 to 0.0625
Outputs:
- grad_input: bfloat16 [512, 16384], P('col', 'row')
- grad_gate: bfloat16 [16384, 8192], P('row', 'col')
- grad_up: bfloat16 [16384, 8192], P('row', 'col')
- grad_down: bfloat16 [8192, 16384], P('col', 'row')
All inputs are finite; a program needn't handle non-finite values.
Results may differ from a plain program's by a relative error of at most 0.005.
Values may be sent and summed in bfloat16 or wider, within the bound.
A program may use at most 128 MiB of HBM per device.

v0:
```python
import jax
import jax.numpy as jnp
from jax import lax
from jax.sharding import PartitionSpec as P


def swiglu_grads(grad_hidden, gate_pre, up_pre):
    gate_val = gate_pre.astype(jnp.float32)
    up_val = up_pre.astype(jnp.float32)
    sigma = 1.0 / (1.0 + jnp.exp(-gate_val))
    grad_gate_pre = (grad_hidden * up_val * sigma * (1.0 + gate_val * (1.0 - sigma))).astype(
        jnp.bfloat16
    )
    grad_up_pre = (grad_hidden * gate_val * sigma).astype(jnp.bfloat16)
    return (grad_gate_pre, grad_up_pre)


def hidden_value(gate_pre, up_pre):
    gate_val = gate_pre.astype(jnp.float32)
    sigma = 1.0 / (1.0 + jnp.exp(-gate_val))
    return (gate_val * sigma * up_pre.astype(jnp.float32)).astype(jnp.bfloat16)


def local(activations, grad_output, gate_pre, up_pre, w_gate, w_up, w_down):
    contract_cols = (((1,), (1,)), ((), ()))
    contract_rows = (((0,), (0,)), ((), ()))
    acts_whole, grad_whole = (
        lax.all_gather(activations, "col", axis=0, tiled=True),
        lax.all_gather(grad_output, "col", axis=0, tiled=True),
    )
    gate_all, up_all = (
        lax.all_gather(gate_pre, "row", axis=0, tiled=True),
        lax.all_gather(up_pre, "row", axis=0, tiled=True),
    )
    partial_hidden = lax.dot_general(
        grad_whole, w_down, contract_cols, preferred_element_type=jnp.float32
    )
    grad_hidden = lax.psum(partial_hidden, "row")
    hidden_all = hidden_value(gate_all, up_all)
    gate_grad_all, up_grad_all = swiglu_grads(grad_hidden, gate_all, up_all)
    grad_down = lax.dot_general(
        hidden_all, grad_whole, contract_rows, preferred_element_type=jnp.float32
    ).astype(jnp.bfloat16)
    grad_gate = lax.dot_general(
        acts_whole, gate_grad_all, contract_rows, preferred_element_type=jnp.float32
    ).astype(jnp.bfloat16)
    grad_up = lax.dot_general(
        acts_whole, up_grad_all, contract_rows, preferred_element_type=jnp.float32
    ).astype(jnp.bfloat16)
    total = lax.dot_general(
        gate_grad_all, w_gate, contract_cols, preferred_element_type=jnp.float32
    )
    grad_input = lax.psum_scatter(
        total
        + lax.dot_general(up_grad_all, w_up, contract_cols, preferred_element_type=jnp.float32),
        "col",
        scatter_dimension=0,
        tiled=True,
    ).astype(jnp.bfloat16)
    return (grad_input, grad_gate, grad_up, grad_down)


def solution(mesh):
    in_specs = (
        P("col", "row"),
        P("col", "row"),
        P("row", "col"),
        P("row", "col"),
        P("row", "col"),
        P("row", "col"),
        P("col", "row"),
    )
    out_specs = (P("col", "row"), P("row", "col"), P("row", "col"), P("col", "row"))
    return jax.shard_map(local, mesh=mesh, in_specs=in_specs, out_specs=out_specs, check_vma=False)
```

profile of v0, /device:TPU:0, one launch (start us, length us, event | category | flops | bytes accessed | tf_op | source)
XLA Modules:
  0.0 335.6 jit_solution(11636700037328227497)
XLA Ops:
  7.2 0.0 all-gather.5.cloned.1.call-start
  7.2 0.7 all-gather.5.cloned.1.call-update
  7.9 0.0 all-gather.9.cloned.1.call-start
  7.9 0.7 all-gather.9.cloned.1.call-update
  8.6 0.0 all-gather.7.cloned.1.call-start
  8.7 0.7 all-gather.7.cloned.1.call-update
  9.4 0.0 all-reduce.2.cloned.1.call-start
  9.4 49.8 %all-gather.5.cloned.1.call-done = bf16[512,4096]{1,0:T(8,128)(2,1)} async-done(((bf16[64,4096]{1,0:T(8,128)(2,1)}), bf16[512,4096]{1,0:T(8,128)(2,1)}) %all-gather.5.cloned.1.call-update) | async-done | bytes 4194320 | tf_op jit(solution)/shard_map/all_gather | solution.py:29
  59.2 10.5 %fusion.15 = f32[512,1024]{1,0:T(8,128)} fusion(bf16[512,4096]{1,0:T(8,128)(2,1)} %all-gather.5.cloned.1.call-done, bf16[1024,4096]{1,0:T(8,128)(2,1)} %param.13), kind=kOutput, calls=%fused_computation.22 | convolution fusion | flops 4294967296 | bytes 14680064 | tf_op jit(solution)/shard_map/dot_general | solution.py:35
  69.7 0.0 all-reduce.2.cloned.1.call-update
  69.7 0.0 all-gather.11.cloned.1.call-start
  69.8 0.5 all-gather.11.cloned.1.call-update
  70.3 0.0 reduce-scatter.2.cloned.1.call-start
  70.4 16.0 %all-gather.9.cloned.1.call-done = bf16[512,1024]{1,0:T(8,128)(2,1)} async-done(((bf16[128,1024]{1,0:T(8,128)(2,1)}), bf16[512,1024]{1,0:T(8,128)(2,1)}) %all-gather.9.cloned.1.call-update) | async-done | bytes 1048592 | tf_op jit(solution)/shard_map/all_gather | solution.py:32
  86.4 28.4 %all-gather.7.cloned.1.call-done = bf16[512,1024]{1,0:T(8,128)(2,1)} async-done(((bf16[128,1024]{1,0:T(8,128)(2,1)}), bf16[512,1024]{1,0:T(8,128)(2,1)}) %all-gather.7.cloned.1.call-update) | async-done | bytes 1048592 | tf_op jit(solution)/shard_map/all_gather | solution.py:33
  114.8 73.0 %all-reduce.2.cloned.1.call-done = f32[512,1024]{1,0:T(8,128)} async-done(((f32[512,1024]{1,0:T(8,128)}), f32[512,1024]{1,0:T(8,128)}) %all-reduce.2.cloned.1.call-update) | async-done | bytes 2097168 | tf_op jit(solution)/shard_map/psum | solution.py:38
  187.8 3.1 fusion.2
  190.9 0.0 copy-start.2
  190.9 1.0 copy-done.2
  191.9 0.0 copy-start
  191.9 0.0 copy-start.1
  191.9 10.3 %fusion.16 = f32[512,4096]{1,0:T(8,128)} fusion(bf16[512,1024]{1,0:T(8,128)(2,1)S(1)} %fusion.2, bf16[4096,1024]{1,0:T(8,128)(2,1)} %param.11), kind=kOutput, calls=%fused_computation.23 | convolution fusion | flops 4294967296 | bytes 17825792 | tf_op jit(solution)/shard_map/dot_general | solution.py:50
  202.1 0.0 copy-done
  202.2 0.0 copy-done.1
  202.2 11.7 %convolution_add_fusion = f32[512,4096]{1,0:T(8,128)} fusion(f32[512,4096]{1,0:T(8,128)} %fusion.16, bf16[4096,1024]{1,0:T(8,128)(2,1)} %param.12, f32[512,1024]{1,0:T(8,128)S(1)} %copy-done, bf16[512,1024]{1,0:T(8,128)(2,1)S(1)} %copy-done.1), kind=kOutput, calls=%fused_computation.3 | convolution fusion | flops 4300734464 | bytes 28311552 | tf_op jit(solution)/shard_map/dot_general | solution.py:55
  213.8 0.0 reduce-scatter.2.cloned.1.call-update
  213.9 10.7 %convolution_convert_fusion = bf16[1024,4096]{1,0:T(8,128)(2,1)} fusion(bf16[512,4096]{1,0:T(8,128)(2,1)} %all-gather.5.cloned.1.call-done, bf16[512,1024]{1,0:T(8,128)(2,1)} %all-gather.7.cloned.1.call-done, bf16[512,1024]{1,0:T(8,128)(2,1)S(1)} %copy-done.1), kind=kOutput, calls=%fused_computation.2 | convolution fusion | flops 4303355904 | bytes 14680064 | tf_op jit(solution)/shard_map/dot_general | solution.py:41
  224.5 11.6 %all-gather.11.cloned.1.call-done = bf16[512,4096]{1,0:T(8,128)(2,1)} async-done(((bf16[64,4096]{1,0:T(8,128)(2,1)}), bf16[512,4096]{1,0:T(8,128)(2,1)}) %all-gather.11.cloned.1.call-update) | async-done | bytes 4194320 | tf_op jit(solution)/shard_map/all_gather | solution.py:28
  236.1 10.5 %convert_bitcast_fusion.1 = bf16[4096,1024]{0,1:T(8,128)(2,1)} fusion(bf16[512,1024]{1,0:T(8,128)(2,1)} %copy-done.2, bf16[512,4096]{1,0:T(8,128)(2,1)} %all-gather.11.cloned.1.call-done), kind=kOutput, calls=%fused_computation.1 | convolution fusion | flops 4299161600 | bytes 13631488 | tf_op jit(solution)/shard_map/dot_general | solution.py:44
  246.6 12.0 %copy.11 = bf16[4096,1024]{1,0:T(8,128)(2,1)} copy(bf16[4096,1024]{0,1:T(8,128)(2,1)} %convert_bitcast_fusion.1) | data formatting | bytes 16777216
  258.6 9.1 %convert_bitcast_fusion = bf16[4096,1024]{0,1:T(8,128)(2,1)} fusion(bf16[512,4096]{1,0:T(8,128)(2,1)} %all-gather.11.cloned.1.call-done, f32[512,1024]{1,0:T(8,128)S(1)} %copy-done, bf16[512,1024]{1,0:T(8,128)(2,1)S(1)} %copy-done.1), kind=kOutput, calls=%fused_computation | convolution fusion | flops 4302831616 | bytes 15728640 | tf_op jit(solution)/shard_map/dot_general | solution.py:47
  267.7 12.0 %copy.12 = bf16[4096,1024]{1,0:T(8,128)(2,1)} copy(bf16[4096,1024]{0,1:T(8,128)(2,1)} %convert_bitcast_fusion) | data formatting | bytes 16777216
  279.7 47.0 %reduce-scatter.2.cloned.1.call-done = f32[64,4096]{1,0:T(8,128)} async-done(((f32[512,4096]{1,0:T(8,128)}), f32[64,4096]{1,0:T(8,128)}) %reduce-scatter.2.cloned.1.call-update) | async-done | bytes 1048592 | tf_op jit(solution)/shard_map/reduce_scatter | solution.py:53
  326.7 2.1 convert_element_type.39
Async XLA Ops:
  7.2 52.0 %all-gather.5.cloned.1.call-start = ((), (), s32[]{:S(2)}) async-start(), calls=%async_computation.1 | async-start | bytes 4718592 | tf_op jit(solution)/shard_map/all_gather | solution.py:29
  7.9 78.5 %all-gather.9.cloned.1.call-start = ((), (), s32[]{:S(2)}) async-start(), calls=%async_computation.4 | async-start | bytes 1310720 | tf_op jit(solution)/shard_map/all_gather | solution.py:32
  8.6 106.1 %all-gather.7.cloned.1.call-start = ((), (), s32[]{:S(2)}) async-start(), calls=%async_computation.3 | async-start | bytes 1310720 | tf_op jit(solution)/shard_map/all_gather | solution.py:33
  9.4 178.4 %all-reduce.2.cloned.1.call-start = ((), (), s32[]{:S(2)}) async-start(), calls=%async_computation.2 | async-start | bytes 4194304 | tf_op jit(solution)/shard_map/psum | solution.py:38
  69.7 166.4 %all-gather.11.cloned.1.call-start = ((), (), s32[]{:S(2)}) async-start(), calls=%async_computation.6 | async-start | bytes 4718592 | tf_op jit(solution)/shard_map/all_gather | solution.py:28
  70.3 256.3 %reduce-scatter.2.cloned.1.call-start = ((), (), s32[]{:S(2)}) async-start(), calls=%async_computation.5 | async-start | bytes 9437184 | tf_op jit(solution)/shard_map/reduce_scatter | solution.py:53
  190.9 1.0 copy-start.2
  191.9 10.3 %copy-start = (f32[512,1024]{1,0:T(8,128)S(1)}, f32[512,1024]{1,0:T(8,128)}, u32[]{:S(2)}) copy-start(f32[512,1024]{1,0:T(8,128)} %all-reduce.2.cloned.1.call-done) | copy-start | bytes 6291460
  191.9 10.3 %copy-start.1 = (bf16[512,1024]{1,0:T(8,128)(2,1)S(1)}, bf16[512,1024]{1,0:T(8,128)(2,1)}, u32[]{:S(2)}) copy-start(bf16[512,1024]{1,0:T(8,128)(2,1)} %all-gather.9.cloned.1.call-done) | copy-start | bytes 3145732
Sparse Core Ops, SparseCore 0:
  9.6 49.5 all-gather.4
  61.0 25.2 all-gather.8
  88.2 26.4 all-gather.6
  118.3 69.4 all-reduce.1
  189.2 46.8 all-gather.10
  238.3 88.3 reduce-scatter.1
where the time goes:
time: 336 us
  waiting for transfers between devices  228 us (68%)
  matrix products  62.7 us (19%)
  local copies, waits for them, and re-layouts  24.9 us (7%)
  between operations  14.1 us (4%)
  other arithmetic  5.15 us (2%)
    psum x1, waiting for transfers between devices, local(): grad_hidden = lax.psum(partial_hidden, 'row')  73 us
    all_gather x1, waiting for transfers between devices, local(): lax.all_gather(grad_output, 'col', axis=0, tiled=True)  49.8 us
    reduce_scatter x1, waiting for transfers between devices, local(): lax.psum_scatter(total + lax.dot_general(up_grad_all, w_up, contract_cols...  47 us
    all_gather x1, waiting for transfers between devices, local(): lax.all_gather(up_pre, 'row', axis=0, tiled=True)  28.4 us
    unnamed x8, local copies, waits for them, and re-layouts  24.9 us
    all_gather x1, waiting for transfers between devices, local(): lax.all_gather(gate_pre, 'row', axis=0, tiled=True)  16 us
    dot_general x1, matrix products, local(): lax.dot_general(up_grad_all, w_up, contract_cols, preferred_element_type=...  11.7 us
    all_gather x1, waiting for transfers between devices, local(): lax.all_gather(activations, 'col', axis=0, tiled=True)  11.6 us
  transfers between devices with their start and end apart: 6, of which 6 were waited for; matrix products, arithmetic and copies ran while one was open for 27% of the time, Pallas kernels for 0%

commit v1 on v0

--- a/solution.py
+++ b/solution.py
@@ -35,7 +35,7 @@
     partial_hidden = lax.dot_general(
         grad_whole, w_down, contract_cols, preferred_element_type=jnp.float32
     )
-    grad_hidden = lax.psum(partial_hidden, "row")
+    grad_hidden = jnp.sum(lax.all_gather(partial_hidden, "row"), axis=0)
     hidden_all = hidden_value(gate_all, up_all)
     gate_grad_all, up_grad_all = swiglu_grads(grad_hidden, gate_all, up_all)
     grad_down = lax.dot_general(

time: 336 us -> 361 us (1.074)
  waiting for transfers between devices: 228 us -> 250 us
  other arithmetic: 5.15 us -> 9.08 us
    all_gather x0 -> x1, waiting for transfers between devices: none -> 84.5 us  [local(): grad_hidden = jnp.sum(lax.all_gather(partial_hidden, 'row'), axis=0)]
    psum x1 -> x0, waiting for transfers between devices: 73 us -> none  [local(): grad_hidden = lax.psum(partial_hidden, 'row')]
    all_gather x1, waiting for transfers between devices: 16 us -> 23.8 us  [local(): lax.all_gather(gate_pre, 'row', axis=0, tiled=True)]
    reduce_sum x0 -> x1, other arithmetic: none -> 4.57 us  [local(): grad_hidden = jnp.sum(lax.all_gather(partial_hidden, 'row'), axis=0)]
    unnamed x8 -> x6, local copies, waits for them, and re-layouts: 24.9 us -> 24.9 us
  transfers between devices with their start and end apart: 6 -> 6, of which waited for: 6 -> 6; matrix products, arithmetic and copies ran while one was open for 27% -> 23% of each run, Pallas kernels for 0% -> 0%
where the time goes in v1:
time: 361 us
  waiting for transfers between devices  250 us (69%)
  matrix products  62.7 us (17%)
  local copies, waits for them, and re-layouts  24.9 us (7%)
  between operations  14.1 us (4%)
  other arithmetic  9.08 us (3%)
    all_gather x1, waiting for transfers between devices, local(): grad_hidden = jnp.sum(lax.all_gather(partial_hidden, 'row'), axis=0)  84.5 us
    all_gather x1, waiting for transfers between devices, local(): lax.all_gather(grad_output, 'col', axis=0, tiled=True)  51.3 us
    reduce_scatter x1, waiting for transfers between devices, local(): lax.psum_scatter(total + lax.dot_general(up_grad_all, w_up, contract_cols...  47 us
    all_gather x1, waiting for transfers between devices, local(): lax.all_gather(up_pre, 'row', axis=0, tiled=True)  28.2 us
    unnamed x6, local copies, waits for them, and re-layouts  24.9 us
    all_gather x1, waiting for transfers between devices, local(): lax.all_gather(gate_pre, 'row', axis=0, tiled=True)  23.8 us
    all_gather x1, waiting for transfers between devices, local(): lax.all_gather(activations, 'col', axis=0, tiled=True)  12.3 us
    dot_general x1, matrix products, local(): lax.dot_general(up_grad_all, w_up, contract_cols, preferred_element_type=...  11.6 us
  transfers between devices with their start and end apart: 6, of which 6 were waited for; matrix products, arithmetic and copies ran while one was open for 23% of the time, Pallas kernels for 0%

profile of v1, /device:TPU:0, one launch (start us, length us, event | category | flops | bytes accessed | tf_op | source)
XLA Modules:
  0.0 360.5 jit_solution(9212546418210119968)
XLA Ops:
  7.2 0.0 all-gather.7.cloned.1.call-start
  7.2 0.7 all-gather.7.cloned.1.call-update
  7.9 0.0 all-gather.15.cloned.1.call-start
  7.9 51.3 %all-gather.7.cloned.1.call-done = bf16[512,4096]{1,0:T(8,128)(2,1)} async-done(((bf16[64,4096]{1,0:T(8,128)(2,1)}), bf16[512,4096]{1,0:T(8,128)(2,1)}) %all-gather.7.cloned.1.call-update) | async-done | bytes 4194320 | tf_op jit(solution)/shard_map/all_gather | solution.py:29
  59.2 10.5 %fusion.15 = f32[512,1024]{1,0:T(8,128)} fusion(bf16[512,4096]{1,0:T(8,128)(2,1)} %all-gather.7.cloned.1.call-done, bf16[1024,4096]{1,0:T(8,128)(2,1)} %param.13), kind=kOutput, calls=%fused_computation.22 | convolution fusion | flops 4294967296 | bytes 14680064 | tf_op jit(solution)/shard_map/dot_general | solution.py:35
  69.7 0.0 all-gather.15.cloned.1.call-update
  69.7 0.0 all-gather.11.cloned.1.call-start
  69.8 0.7 all-gather.11.cloned.1.call-update
  70.5 0.0 all-gather.9.cloned.1.call-start
  70.5 0.5 all-gather.9.cloned.1.call-update
  71.0 0.0 all-gather.13.cloned.1.call-start
  71.1 0.5 all-gather.13.cloned.1.call-update
  71.6 0.0 reduce-scatter.2.cloned.1.call-start
  71.7 84.5 %all-gather.15.cloned.1.call-done = f32[2048,1024]{1,0:T(8,128)} async-done(((f32[512,1024]{1,0:T(8,128)}), f32[2048,1024]{1,0:T(8,128)}) %all-gather.15.cloned.1.call-update) | async-done | bytes 8388624 | tf_op jit(solution)/shard_map/all_gather | solution.py:38
  156.2 4.6 %reduce_sum.9 = f32[512,1024]{1,0:T(8,128)S(1)} reduce(f32[4,512,1024]{2,1,0:T(8,128)} %bitcast.14, f32[]{:T(128)} %constant.0.clone.1), dimensions={0}, to_apply=%region_0.0 | reduce | flops 1572864 | bytes 10485764 | tf_op jit(solution)/shard_map/reduce_sum | solution.py:38
  160.7 23.8 %all-gather.11.cloned.1.call-done = bf16[512,1024]{1,0:T(8,128)(2,1)} async-done(((bf16[128,1024]{1,0:T(8,128)(2,1)}), bf16[512,1024]{1,0:T(8,128)(2,1)}) %all-gather.11.cloned.1.call-update) | async-done | bytes 1048592 | tf_op jit(solution)/shard_map/all_gather | solution.py:32
  184.5 28.2 %all-gather.9.cloned.1.call-done = bf16[512,1024]{1,0:T(8,128)(2,1)} async-done(((bf16[128,1024]{1,0:T(8,128)(2,1)}), bf16[512,1024]{1,0:T(8,128)(2,1)}) %all-gather.9.cloned.1.call-update) | async-done | bytes 1048592 | tf_op jit(solution)/shard_map/all_gather | solution.py:33
  212.8 2.4 fusion.2
  215.2 0.0 copy-start.1
  215.2 1.0 copy-done.1
  216.2 0.0 copy-start
  216.2 10.2 %fusion.16 = f32[512,4096]{1,0:T(8,128)} fusion(bf16[512,1024]{1,0:T(8,128)(2,1)S(1)} %fusion.2, bf16[4096,1024]{1,0:T(8,128)(2,1)} %param.11), kind=kOutput, calls=%fused_computation.23 | convolution fusion | flops 4294967296 | bytes 17825792 | tf_op jit(solution)/shard_map/dot_general | solution.py:50
  226.4 0.0 copy-done
  226.4 11.6 %convolution_add_fusion = f32[512,4096]{1,0:T(8,128)} fusion(f32[512,4096]{1,0:T(8,128)} %fusion.16, bf16[4096,1024]{1,0:T(8,128)(2,1)} %param.12, f32[512,1024]{1,0:T(8,128)S(1)} %reduce_sum.9, bf16[512,1024]{1,0:T(8,128)(2,1)S(1)} %copy-done), kind=kOutput, calls=%fused_computation.3 | convolution fusion | flops 4300734464 | bytes 28311552 | tf_op jit(solution)/shard_map/dot_general | solution.py:55
  238.1 0.0 reduce-scatter.2.cloned.1.call-update
  238.1 10.7 %convolution_convert_fusion = bf16[1024,4096]{1,0:T(8,128)(2,1)} fusion(bf16[512,4096]{1,0:T(8,128)(2,1)} %all-gather.7.cloned.1.call-done, bf16[512,1024]{1,0:T(8,128)(2,1)} %all-gather.9.cloned.1.call-done, bf16[512,1024]{1,0:T(8,128)(2,1)S(1)} %copy-done), kind=kOutput, calls=%fused_computation.2 | convolution fusion | flops 4303355904 | bytes 14680064 | tf_op jit(solution)/shard_map/dot_general | solution.py:41
  248.8 12.3 %all-gather.13.cloned.1.call-done = bf16[512,4096]{1,0:T(8,128)(2,1)} async-done(((bf16[64,4096]{1,0:T(8,128)(2,1)}), bf16[512,4096]{1,0:T(8,128)(2,1)}) %all-gather.13.cloned.1.call-update) | async-done | bytes 4194320 | tf_op jit(solution)/shard_map/all_gather | solution.py:28
  261.1 10.5 %convert_bitcast_fusion.1 = bf16[4096,1024]{0,1:T(8,128)(2,1)} fusion(bf16[512,1024]{1,0:T(8,128)(2,1)} %copy-done.1, bf16[512,4096]{1,0:T(8,128)(2,1)} %all-gather.13.cloned.1.call-done), kind=kOutput, calls=%fused_computation.1 | convolution fusion | flops 4299161600 | bytes 13631488 | tf_op jit(solution)/shard_map/dot_general | solution.py:44
  271.6 12.0 %copy.11 = bf16[4096,1024]{1,0:T(8,128)(2,1)} copy(bf16[4096,1024]{0,1:T(8,128)(2,1)} %convert_bitcast_fusion.1) | data formatting | bytes 16777216
  283.5 9.1 %convert_bitcast_fusion = bf16[4096,1024]{0,1:T(8,128)(2,1)} fusion(bf16[512,4096]{1,0:T(8,128)(2,1)} %all-gather.13.cloned.1.call-done, f32[512,1024]{1,0:T(8,128)S(1)} %reduce_sum.9, bf16[512,1024]{1,0:T(8,128)(2,1)S(1)} %copy-done), kind=kOutput, calls=%fused_computation | convolution fusion | flops 4302831616 | bytes 15728640 | tf_op jit(solution)/shard_map/dot_general | solution.py:47
  292.7 12.0 %copy.12 = bf16[4096,1024]{1,0:T(8,128)(2,1)} copy(bf16[4096,1024]{0,1:T(8,128)(2,1)} %convert_bitcast_fusion) | data formatting | bytes 16777216
  304.6 47.0 %reduce-scatter.2.cloned.1.call-done = f32[64,4096]{1,0:T(8,128)} async-done(((f32[512,4096]{1,0:T(8,128)}), f32[64,4096]{1,0:T(8,128)}) %reduce-scatter.2.cloned.1.call-update) | async-done | bytes 1048592 | tf_op jit(solution)/shard_map/reduce_scatter | solution.py:53
  351.6 2.1 convert_element_type.39
Async XLA Ops:
  7.2 52.0 %all-gather.7.cloned.1.call-start = ((), (), s32[]{:S(2)}) async-start(), calls=%async_computation.1 | async-start | bytes 4718592 | tf_op jit(solution)/shard_map/all_gather | solution.py:29
  7.9 148.3 %all-gather.15.cloned.1.call-start = ((), (), s32[]{:S(2)}) async-start(), calls=%async_computation.6 | async-start | bytes 10485760 | tf_op jit(solution)/shard_map/all_gather | solution.py:38
  69.7 114.8 %all-gather.11.cloned.1.call-start = ((), (), s32[]{:S(2)}) async-start(), calls=%async_computation.3 | async-start | bytes 1310720 | tf_op jit(solution)/shard_map/all_gather | solution.py:32
  70.5 142.3 %all-gather.9.cloned.1.call-start = ((), (), s32[]{:S(2)}) async-start(), calls=%async_computation.2 | async-start | bytes 1310720 | tf_op jit(solution)/shard_map/all_gather | solution.py:33
  71.0 190.1 %all-gather.13.cloned.1.call-start = ((), (), s32[]{:S(2)}) async-start(), calls=%async_computation.5 | async-start | bytes 4718592 | tf_op jit(solution)/shard_map/all_gather | solution.py:28
  71.6 280.0 %reduce-scatter.2.cloned.1.call-start = ((), (), s32[]{:S(2)}) async-start(), calls=%async_computation.4 | async-start | bytes 9437184 | tf_op jit(solution)/shard_map/reduce_scatter | solution.py:53
  215.2 1.0 copy-start.1
  216.2 10.2 %copy-start = (bf16[512,1024]{1,0:T(8,128)(2,1)S(1)}, bf16[512,1024]{1,0:T(8,128)(2,1)}, u32[]{:S(2)}) copy-start(bf16[512,1024]{1,0:T(8,128)(2,1)} %all-gather.11.cloned.1.call-done) | copy-start | bytes 3145732
Sparse Core Ops, SparseCore 0:
  9.6 49.5 all-gather.6
  69.8 86.2 all-gather.14
  158.0 26.4 all-gather.10
  186.2 26.4 all-gather.8
  214.2 46.8 all-gather.12
  263.3 88.3 reduce-scatter.1
